TPU v7x, 512 devices: a whole 4x4x16 slice. The times are simulated.
512 devices in a mesh: kv: 8 (over x, core), pool: 64 (over y, z).
Axes of the slice: x: 4, y: 4, z: 16, core: 2. Of those that a mesh axis runs over, the one named last changes fastest.
Arguments:
- hidden: bfloat16 [64, 2048], P('pool'), may hold values from -6 to 6
- norm_attn: bfloat16 [2048], replicated, may hold values from 0.099609375 to 1.8984375
- wq: bfloat16 [2048, 2048], P(None, 'kv'), may hold values from -0.125 to 0.125
- wkv: bfloat16 [2, 2048, 1024], P(None, None, 'kv'), may hold values from -0.125 to 0.125
- wo: bfloat16 [2048, 2048], P('kv'), may hold values from -0.125 to 0.125
- cache: bfloat16 [2, 1024, 128, 1024], P(None, 'pool', None, 'kv'), may hold values from -70 to 70, as said below
- slot_entry: int32 [1024], P('pool'), may hold values from -1 to 4095, as said below
- lengths: int32 [64], replicated, may hold values from 1 to 8192, as said below
- norm_mlp: bfloat16 [2048], replicated, may hold values from 0.099609375 to 1.8984375
- w_gate: bfloat16 [2048, 8192], P('pool', 'kv'), may hold values from -0.125 to 0.125
- w_up: bfloat16 [2048, 8192], P('pool', 'kv'), may hold values from -0.125 to 0.125
- w_down: bfloat16 [8192, 2048], P('kv', 'pool'), may hold values from -0.0625 to 0.0625
Outputs:
- output: bfloat16 [64, 2048], P('pool')
Inputs may be any that keep to these rules, and one draw needn't show every extreme that they name: slot_entry[s] is -1 for a free slot, else r * 64 + b: the slot holds block b of request r, that is its cached positions b * 128 to b * 128 + 127 that lie below lengths[r]. Every block of every request below ceil(lengths[r] / 128) sits in exactly one slot, anywhere in the pool; a holder's slots are its 16 entries. Its new token stands at position lengths[r]. `cache`: keys and values of the cached tokens, already rotated.
All inputs are finite; a program needn't handle non-finite values.
Results may differ from a plain program's by a relative error of at most 0.012.
The roundings to bfloat16 on the way count: a program that leaves them out, or rounds other values in their place, can miss the bound.
Values may be sent and summed in bfloat16 or wider, within the bound.
A program may use at most 64 MiB of HBM per device.

v0:
```python
import math
import jax
import jax.numpy as jnp
from jax import lax
from jax.sharding import PartitionSpec as P

QUERY_HEAD_COUNT = 16
KEY_VALUE_HEADS = 8
HEAD_SIZE = 128
NEGATIVE = -1e30
EPSILON = 1e-05
ROPE_BASE = 1000000.0


def narrow_rows(tensor):
    return lax.optimization_barrier(tensor.astype(jnp.bfloat16))


def rms_scale(inputs, gain_vec):
    widened = inputs.astype(jnp.float32)
    mean_square = jnp.mean(widened * widened, axis=-1, keepdims=True)
    return narrow_rows(widened * lax.rsqrt(mean_square + EPSILON) * gain_vec.astype(jnp.float32))


def rotate(vectors, positions):
    head_width = vectors.shape[-1]
    halfway = head_width // 2
    frequency = jnp.exp(
        jnp.arange(halfway, dtype=jnp.float32) * (-2.0 * math.log(ROPE_BASE) / head_width)
    )
    angles = positions.astype(jnp.float32)[:, None] * frequency[None, :]
    cosine = jnp.cos(angles)[:, None, :]
    sine_of = jnp.sin(angles)[:, None, :]
    leading = vectors[..., :halfway]
    trailing = vectors[..., halfway:]
    return jnp.concatenate(
        [leading * cosine - trailing * sine_of, trailing * cosine + leading * sine_of], axis=-1
    )


def per_device(
    hidden, norm_attn, wq, wkv, wo, cache, slot_entry, lengths, norm_mlp, w_gate, w_up, w_down
):
    home_rows = hidden.shape[0]
    shared_heads = wkv.shape[2] // HEAD_SIZE
    queries_per_shared = QUERY_HEAD_COUNT // KEY_VALUE_HEADS
    query_heads = shared_heads * queries_per_shared
    home_index = lax.axis_index("pool")
    max_blocks = slot_entry.shape[0] * lax.axis_size("pool") // 16
    positions = lax.dynamic_slice_in_dim(lengths, home_index * home_rows, home_rows)
    normed_input = rms_scale(hidden, norm_attn)
    query_rows = jnp.dot(normed_input, wq, preferred_element_type=jnp.float32).reshape(
        home_rows, query_heads, HEAD_SIZE
    )
    query_rows = narrow_rows(rotate(query_rows, positions) * HEAD_SIZE ** (-0.5))
    fresh_keys = jnp.dot(normed_input, wkv[0], preferred_element_type=jnp.float32).reshape(
        home_rows, shared_heads, HEAD_SIZE
    )
    fresh_keys = narrow_rows(rotate(fresh_keys, positions))
    fresh_values = narrow_rows(
        jnp.dot(normed_input, wkv[1], preferred_element_type=jnp.float32)
    ).reshape(home_rows, shared_heads, HEAD_SIZE)
    every_query = lax.all_gather(
        query_rows.reshape(home_rows, query_heads * HEAD_SIZE), "pool", axis=0, tiled=True
    )
    request_list = every_query.shape[0]
    every_query = every_query.reshape(request_list, shared_heads, queries_per_shared, HEAD_SIZE)
    slot_count = slot_entry.shape[0]
    block_len = cache.shape[2]
    live_slot = slot_entry >= 0
    owners = jnp.where(live_slot, slot_entry // max_blocks, 0)
    block_index = jnp.where(live_slot, slot_entry % max_blocks, 0)
    position = block_index[:, None] * block_len + jnp.arange(block_len, dtype=jnp.int32)[None, :]
    in_range = live_slot[:, None] & (position < lengths[owners][:, None])
    token_owner = jnp.where(in_range, owners[:, None], -1).reshape(1, slot_count * block_len)
    keys = cache[0].reshape(slot_count * block_len, HEAD_SIZE)
    values = cache[1].reshape(slot_count * block_len, HEAD_SIZE)
    stacked = every_query.reshape(request_list, query_heads, HEAD_SIZE).transpose(1, 0, 2)
    stacked = stacked.reshape(query_heads * request_list, HEAD_SIZE)
    scores = lax.dot_general(
        stacked, keys, (((1,), (1,)), ((), ())), preferred_element_type=jnp.float32
    )
    row_owner = jnp.tile(jnp.arange(request_list, dtype=jnp.int32), query_heads)[:, None]
    taken = row_owner == token_owner
    scores = jnp.where(taken, scores, NEGATIVE)
    row_max = jnp.max(scores, axis=-1, keepdims=True)
    raised = jnp.where(taken, jnp.exp(scores - row_max), 0.0)
    row_total = jnp.sum(raised, axis=-1, keepdims=True)
    row_out = jnp.dot(raised.astype(jnp.bfloat16), values, preferred_element_type=jnp.float32)
    packed = (
        jnp.concatenate(
            [
                row_out,
                jnp.broadcast_to(row_max, (row_max.shape[0], 64)),
                jnp.broadcast_to(row_total, (row_max.shape[0], 64)),
            ],
            axis=1,
        )
        .reshape(query_heads, request_list, 256)
        .transpose(1, 0, 2)
        .reshape(request_list, query_heads * 256)
    )
    arrived = lax.all_to_all(packed, "pool", split_axis=0, concat_axis=0, tiled=True)
    arrived = arrived.reshape(request_list, query_heads, 256)
    every_max = arrived[:, :, 128]
    part_max = jnp.max(every_max, axis=0, keepdims=True)
    factor = jnp.exp(every_max - part_max)
    part_total = jnp.sum(factor * arrived[:, :, 192], axis=0, keepdims=True)
    part_out = jnp.sum(factor[:, :, None] * arrived[:, :, :128], axis=0).reshape(
        1, query_heads * HEAD_SIZE
    )
    own_query = query_rows.reshape(home_rows, shared_heads, queries_per_shared, HEAD_SIZE).astype(
        jnp.float32
    )
    new_score = jnp.sum(own_query * fresh_keys.astype(jnp.float32)[:, :, None, :], axis=-1).reshape(
        home_rows, query_heads
    )
    highest = jnp.maximum(part_max, new_score)
    old_scale = jnp.exp(part_max - highest)
    new_scale = jnp.exp(new_score - highest)
    weight_sum = part_total * old_scale + new_scale
    new_term = (
        new_scale.reshape(home_rows, shared_heads, queries_per_shared)[..., None]
        * fresh_values.astype(jnp.float32)[:, :, None, :]
    )
    combined = part_out.reshape(home_rows, query_heads, HEAD_SIZE) * old_scale[
        ..., None
    ] + new_term.reshape(home_rows, query_heads, HEAD_SIZE)
    attended = narrow_rows(combined / weight_sum[..., None]).reshape(
        home_rows, query_heads * HEAD_SIZE
    )
    projected = lax.psum(jnp.dot(attended, wo, preferred_element_type=jnp.float32), "kv")
    residual = narrow_rows(hidden.astype(jnp.float32) + projected)
    mlp_in = rms_scale(residual, norm_mlp)
    columns = lax.all_to_all(mlp_in, "pool", split_axis=1, concat_axis=0, tiled=True)
    hidden_width = w_gate.shape[1]
    gate_term = jnp.dot(columns, w_gate, preferred_element_type=jnp.float32)
    up_term = jnp.dot(columns, w_up, preferred_element_type=jnp.float32)
    sent = jnp.concatenate([gate_term, up_term], axis=1).astype(jnp.bfloat16)
    summed = jnp.sum(
        lax.all_to_all(sent, "pool", split_axis=0, concat_axis=0, tiled=True).astype(jnp.float32),
        axis=0,
        keepdims=True,
    )
    activation = narrow_rows(jax.nn.silu(summed[:, :hidden_width]) * summed[:, hidden_width:])
    projected_down = jnp.dot(
        lax.all_gather(activation, "pool", axis=0, tiled=True),
        w_down,
        preferred_element_type=jnp.float32,
    )
    mlp_out = narrow_rows(lax.psum(projected_down, "kv"))
    returned = lax.all_to_all(mlp_out, "pool", split_axis=0, concat_axis=1, tiled=True)
    return (residual.astype(jnp.float32) + returned.astype(jnp.float32)).astype(jnp.bfloat16)


def solution(mesh):
    return jax.shard_map(
        per_device,
        mesh=mesh,
        in_specs=(
            P("pool", None),
            P(),
            P(None, "kv"),
            P(None, None, "kv"),
            P("kv", None),
            P(None, "pool", None, "kv"),
            P("pool"),
            P(),
            P(),
            P("pool", "kv"),
            P("pool", "kv"),
            P("kv", "pool"),
        ),
        out_specs=P("pool", None),
        check_vma=False,
    )
```

profile of v0, /device:TPU:8, one launch (start us, length us, event | category | flops | bytes accessed | tf_op | source)
XLA Modules:
  0.0 311.4 jit_solution(4484563222303054181)
XLA Ops:
  0.0 0.7 copy-done.9
  0.8 0.6 copy-done.1
  1.5 0.6 dynamic_slice.3
  2.8 0.6 multiply_reduce_fusion.1
  4.1 1.5 fusion.4
  5.7 88.1 %all-gather = bf16[64,1,256]{2,1,0:T(2,128)(2,1)S(1)} all-gather(bf16[1,1,256]{2,1,0:T(2,128)(2,1)S(1)} %reshape.500), channel_id=1, replica_groups=mesh['kv'=8,'pool'=64] {'pool'}, dimensions={0}, use_global_device_ids=true | all-gather | bytes 33280 | tf_op jit(solution)/shard_map/all_gather | solution.py:63
  94.1 0.7 gather_fusion
  95.8 0.4 fusion.9
  96.5 0.8 all_to_all.40
  97.3 10.4 %all-to-all-start = ((f32[64,1,512]{2,1,0:T(1,128)}), f32[64,1,512]{2,1,0:T(1,128)S(1)}, u32[]{:S(2)}, u32[]{:S(2)}) async-start(f32[64,1,512]{2,1,0:T(1,128)} %all_to_all.40), calls=%async_computation | async-start | bytes 262144 | tf_op jit(solution)/shard_map/all_to_all | solution.py:103
  108.3 0.5 copy-done.8
  109.0 13.0 %all-to-all-done = f32[64,1,512]{2,1,0:T(1,128)S(1)} async-done(((f32[64,1,512]{2,1,0:T(1,128)}), f32[64,1,512]{2,1,0:T(1,128)S(1)}, u32[]{:S(2)}, u32[]{:S(2)}) %all-to-all-start) | async-done | bytes 131104 | tf_op jit(solution)/shard_map/all_to_all | solution.py:103
  123.6 12.6 %psum.14 = f32[1,2048]{1,0:T(1,128)S(1)} all-reduce(f32[1,2048]{1,0:T(1,128)S(1)} %fusion.53), channel_id=1, replica_groups=mesh['kv'=8,'pool'=64] {'kv'}, use_global_device_ids=true, to_apply=%region_7.8 | all-reduce | flops 2048 | bytes 16384 | tf_op jit(solution)/shard_map/psum | solution.py:132
  136.3 0.6 multiply_reduce_fusion
  137.8 19.7 %all_to_all.46 = bf16[1,64,32]{2,0,1:T(2,128)(2,1)S(1)} all-to-all(bf16[1,64,32]{2,0,1:T(2,128)(2,1)S(1)} %all_to_all.41), channel_id=1, replica_groups=mesh['kv'=8,'pool'=64] {'pool'}, dimensions={1} | all-to-all | bytes 8192 | tf_op jit(solution)/shard_map/all_to_all | solution.py:135
  157.8 0.6 copy-done.6
  158.7 0.5 broadcast.240
  159.2 0.8 reduce.13
  160.1 24.5 %all_to_all.47 = bf16[64,2,1024]{2,1,0:T(2,128)(2,1)S(1)} all-to-all(bf16[64,2,1024]{2,1,0:T(2,128)(2,1)S(1)} %reshape.527), channel_id=1, replica_groups=mesh['kv'=8,'pool'=64] {'pool'}, dimensions={0} | all-to-all | bytes 524288 | tf_op jit(solution)/shard_map/all_to_all | solution.py:141
  184.8 0.5 convert_reduce_fusion
  185.4 80.0 %all-gather.1 = bf16[64,1,1024]{2,1,0:T(2,128)(2,1)S(1)} all-gather(bf16[1,1,1024]{2,1,0:T(2,128)(2,1)S(1)} %bitcast.109), channel_id=1, replica_groups=mesh['kv'=8,'pool'=64] {'pool'}, dimensions={0}, use_global_device_ids=true | all-gather | bytes 133120 | tf_op jit(solution)/shard_map/all_gather | solution.py:147
  265.5 23.6 %psum.15 = bf16[64,32]{0,1:T(8,128)(2,1)S(1)} all-reduce(f32[64,32]{0,1:T(8,128)S(1)} %fusion.19), channel_id=1, replica_groups=mesh['kv'=8,'pool'=64] {'kv'}, use_global_device_ids=true, to_apply=%region_10.11 | all-reduce | flops 2048 | bytes 12288 | tf_op jit(solution)/shard_map/psum | solution.py:151
  289.2 21.4 %all_to_all.48 = bf16[64,1,32]{2,1,0:T(2,128)(2,1)S(1)} all-to-all(bf16[64,1,32]{2,1,0:T(2,128)(2,1)S(1)} %copy.54), channel_id=1, replica_groups=mesh['kv'=8,'pool'=64] {'pool'}, dimensions={0} | all-to-all | bytes 8192 | tf_op jit(solution)/shard_map/all_to_all | solution.py:152
  310.8 0.6 add_convert_fusion
  (77 shorter events, 5.6 us)
Async XLA Ops:
  0.0 123.4 %copy-start = (bf16[256,2048]{1,0:T(8,128)(2,1)S(1)}, bf16[256,2048]{1,0:T(8,128)(2,1)}, u32[]{:S(2)}) copy-start(bf16[256,2048]{1,0:T(8,128)(2,1)} %param.16) | copy-start | bytes 3145732
  0.0 0.7 copy-start.9
  0.7 2.0 copy-start.7
  0.8 2.0 copy-start.4
  0.8 0.7 copy-start.1
  0.8 94.0 %copy-start.3 = (bf16[2,16,128,128]{3,2,1,0:T(8,128)(2,1)S(1)}, bf16[2,16,128,128]{3,2,1,0:T(8,128)(2,1)}, u32[]{:S(2)}) copy-start(bf16[2,16,128,128]{3,2,1,0:T(8,128)(2,1)} %param.17) | copy-start | bytes 3145732
  96.2 11.5 %copy-start.2 = (bf16[2,2048,128]{2,1,0:T(8,128)(2,1)S(1)}, bf16[2,2048,128]{2,1,0:T(8,128)(2,1)}, u32[]{:S(2)}) copy-start(bf16[2,2048,128]{2,1,0:T(8,128)(2,1)} %param.15) | copy-start | bytes 3145732
  97.3 24.6 %all-to-all-start = ((f32[64,1,512]{2,1,0:T(1,128)}), f32[64,1,512]{2,1,0:T(1,128)S(1)}, u32[]{:S(2)}, u32[]{:S(2)}) async-start(f32[64,1,512]{2,1,0:T(1,128)} %all_to_all.40), calls=%async_computation | async-start | bytes 262144 | tf_op jit(solution)/shard_map/all_to_all | solution.py:103
  108.1 0.7 copy-start.8
  137.7 19.9 %copy-start.5 = (bf16[32,1024]{1,0:T(8,128)(2,1)S(1)}, bf16[32,1024]{1,0:T(8,128)(2,1)}, u32[]{:S(2)}) copy-start(bf16[32,1024]{1,0:T(8,128)(2,1)} %param.21) | copy-start | bytes 196612
  157.6 0.9 copy-start.6
  185.3 80.0 %copy-start.10 = (bf16[1024,32]{0,1:T(8,128)(2,1)S(1)}, bf16[1024,32]{0,1:T(8,128)(2,1)}, u32[]{:S(2)}) copy-start(bf16[1024,32]{0,1:T(8,128)(2,1)} %param.23) | copy-start | bytes 196612
where the time goes:
time: 312 us; the launch traced here: 311 us
  blocking collectives  270 us (87%)
  waiting for transfers between devices  13 us (4%)
  starting transfers between devices  10.4 us (3%)
  local copies, waits for them, and re-layouts  6.74 us (2%)
  other arithmetic  5.5 us (2%)
  matrix products  3.47 us (1%)
    all_gather x1, blocking collectives, per_device(): lax.all_gather(query_rows.reshape(home_rows, query_heads * HEAD_SIZE), 'p...  88.1 us
    all_gather x1, blocking collectives, per_device(): lax.all_gather(activation, 'pool', axis=0, tiled=True)  80 us
    all_to_all x1, blocking collectives, per_device(): lax.all_to_all(sent, 'pool', split_axis=0, concat_axis=0, tiled=True)  24.5 us
    psum x1, blocking collectives, per_device(): mlp_out = narrow_rows(lax.psum(projected_down, 'kv'))  23.6 us
    all_to_all x1, blocking collectives, per_device(): lax.all_to_all(mlp_out, 'pool', split_axis=0, concat_axis=1, tiled=True)  21.4 us
    all_to_all x1, blocking collectives, per_device(): lax.all_to_all(mlp_in, 'pool', split_axis=1, concat_axis=0, tiled=True)  19.7 us
    all_to_all x1, waiting for transfers between devices, per_device(): lax.all_to_all(packed, 'pool', split_axis=0, concat_axis=0, tiled=True)  13 us
    psum x1, blocking collectives, per_device(): lax.psum(jnp.dot(attended, wo, preferred_element_type=jnp.float32), 'kv')  12.6 us
  transfers between devices with their start and end apart: 1, of which 1 were waited for; matrix products, arithmetic and copies ran while one was open for 0% of the time, Pallas kernels for 0%

commit v1 on v0

--- a/solution.py
+++ b/solution.py
@@ -10,6 +10,13 @@
 NEGATIVE = -1e30
 EPSILON = 1e-05
 ROPE_BASE = 1000000.0
+
+
+def exchange_gather(value, name, d):
+    devices = lax.axis_size(name)
+    parts = jnp.stack([value for _ in range(devices)])
+    parts = lax.all_to_all(parts, name, split_axis=0, concat_axis=0)
+    return jnp.concatenate(parts, axis=d)
 
 
 def narrow_rows(tensor):
@@ -60,9 +67,7 @@
     fresh_values = narrow_rows(
         jnp.dot(normed_input, wkv[1], preferred_element_type=jnp.float32)
     ).reshape(home_rows, shared_heads, HEAD_SIZE)
-    every_query = lax.all_gather(
-        query_rows.reshape(home_rows, query_heads * HEAD_SIZE), "pool", axis=0, tiled=True
-    )
+    every_query = exchange_gather(query_rows.reshape(home_rows, query_heads * HEAD_SIZE), "pool", 0)
     request_list = every_query.shape[0]
     every_query = every_query.reshape(request_list, shared_heads, queries_per_shared, HEAD_SIZE)
     slot_count = slot_entry.shape[0]

time: 312 us -> 252 us (0.81)
  blocking collectives: 270 us -> 182 us
  starting transfers between devices: 10.4 us -> 24.1 us
  waiting for transfers between devices: 13 us -> 25.9 us
    all_gather x1 -> x0, blocking collectives: 88.1 us -> none  [per_device(): lax.all_gather(query_rows.reshape(home_rows, query_heads * HEAD_SIZE), 'p...]
    all_to_all x0 -> x1, starting transfers between devices: none -> 18.7 us  [exchange_gather(): parts = lax.all_to_all(parts, name, split_axis=0, concat_axis=0)]
    all_to_all x0 -> x1, waiting for transfers between devices: none -> 11.4 us  [exchange_gather(): parts = lax.all_to_all(parts, name, split_axis=0, concat_axis=0)]
    all_to_all x1, starting transfers between devices: 10.4 us -> 5.4 us  [per_device(): lax.all_to_all(packed, 'pool', split_axis=0, concat_axis=0, tiled=True)]
  transfers between devices with their start and end apart: 1 -> 2, of which waited for: 1 -> 2; matrix products, arithmetic and copies ran while one was open for 0% -> 1% of each run, Pallas kernels for 0% -> 0%
where the time goes in v1:
time: 252 us
  blocking collectives  182 us (72%)
  waiting for transfers between devices  25.9 us (10%)
  starting transfers between devices  24.1 us (10%)
  local copies, waits for them, and re-layouts  7.43 us (3%)
  other arithmetic  6.4 us (3%)
  matrix products  3.47 us (1%)
    all_gather x1, blocking collectives, per_device(): lax.all_gather(activation, 'pool', axis=0, tiled=True)  80.1 us
    psum x1, blocking collectives, per_device(): mlp_out = narrow_rows(lax.psum(projected_down, 'kv'))  23.6 us
    all_to_all x1, blocking collectives, per_device(): lax.all_to_all(sent, 'pool', split_axis=0, concat_axis=0, tiled=True)  23.5 us
    all_to_all x1, blocking collectives, per_device(): lax.all_to_all(mlp_out, 'pool', split_axis=0, concat_axis=1, tiled=True)  21.3 us
    all_to_all x1, blocking collectives, per_device(): lax.all_to_all(mlp_in, 'pool', split_axis=1, concat_axis=0, tiled=True)  20.6 us
    all_to_all x1, starting transfers between devices, exchange_gather(): parts = lax.all_to_all(parts, name, split_axis=0, concat_axis=0)  18.7 us
    all_to_all x1, waiting for transfers between devices, per_device(): lax.all_to_all(packed, 'pool', split_axis=0, concat_axis=0, tiled=True)  14.5 us
    psum x1, blocking collectives, per_device(): lax.psum(jnp.dot(attended, wo, preferred_element_type=jnp.float32), 'kv')  12.6 us
  transfers between devices with their start and end apart: 2, of which 2 were waited for; matrix products, arithmetic and copies ran while one was open for 1% of the time, Pallas kernels for 0%

profile of v1, /device:TPU:8, one launch (start us, length us, event | category | flops | bytes accessed | tf_op | source)
XLA Modules:
  0.0 251.6 jit_solution(14879176266495623159)
XLA Ops:
  0.0 0.8 copy-done.4
  0.8 0.6 multiply_reduce_fusion.1
  2.1 0.6 copy-done.1
  2.8 0.6 dynamic_slice.3
  4.1 1.5 fusion.4
  6.3 0.8 reduce.13
  7.1 0.6 reshape.523
  7.8 18.7 %all-to-all-start = ((bf16[64,2,128]{2,1,0:T(2,128)(2,1)}), bf16[64,2,128]{2,1,0:T(2,128)(2,1)S(1)}, u32[]{:S(2)}, u32[]{:S(2)}) async-start(bf16[64,2,128]{2,1,0:T(2,128)(2,1)} %reshape.523), calls=%async_computation | async-start | bytes 65536 | tf_op jit(solution)/shard_map/all_to_all | solution.py:18
  27.0 0.7 gather_fusion
  27.8 0.5 copy-done.8
  28.6 11.4 %all-to-all-done = bf16[64,2,128]{2,1,0:T(2,128)(2,1)S(1)} async-done(((bf16[64,2,128]{2,1,0:T(2,128)(2,1)}), bf16[64,2,128]{2,1,0:T(2,128)(2,1)S(1)}, u32[]{:S(2)}, u32[]{:S(2)}) %all-to-all-start) | async-done | bytes 32800 | tf_op jit(solution)/shard_map/all_to_all | solution.py:18
  41.7 0.8 all_to_all.44
  42.5 5.4 %all-to-all-start.1 = ((f32[64,1,512]{2,1,0:T(1,128)}), f32[64,1,512]{2,1,0:T(1,128)S(1)}, u32[]{:S(2)}, u32[]{:S(2)}) async-start(f32[64,1,512]{2,1,0:T(1,128)} %all_to_all.44), calls=%async_computation.1 | async-start | bytes 262144 | tf_op jit(solution)/shard_map/all_to_all | solution.py:108
  48.0 14.5 %all-to-all-done.1 = f32[64,1,512]{2,1,0:T(1,128)S(1)} async-done(((f32[64,1,512]{2,1,0:T(1,128)}), f32[64,1,512]{2,1,0:T(1,128)S(1)}, u32[]{:S(2)}, u32[]{:S(2)}) %all-to-all-start.1) | async-done | bytes 131104 | tf_op jit(solution)/shard_map/all_to_all | solution.py:108
  64.2 12.6 %psum.14 = f32[1,2048]{1,0:T(1,128)S(1)} all-reduce(f32[1,2048]{1,0:T(1,128)S(1)} %fusion.53), channel_id=1, replica_groups=mesh['kv'=8,'pool'=64] {'kv'}, use_global_device_ids=true, to_apply=%region_7.8 | all-reduce | flops 2048 | bytes 16384 | tf_op jit(solution)/shard_map/psum | solution.py:137
  76.9 0.7 multiply_reduce_fusion
  78.5 20.6 %all_to_all.51 = bf16[1,64,32]{2,0,1:T(2,128)(2,1)S(1)} all-to-all(bf16[1,64,32]{2,0,1:T(2,128)(2,1)S(1)} %all_to_all.45), channel_id=1, replica_groups=mesh['kv'=8,'pool'=64] {'pool'}, dimensions={1} | all-to-all | bytes 8192 | tf_op jit(solution)/shard_map/all_to_all | solution.py:140
  99.4 0.6 copy-done.6
  100.3 0.8 reduce.14
  101.2 23.5 %all_to_all.52 = bf16[64,2,1024]{2,1,0:T(2,128)(2,1)S(1)} all-to-all(bf16[64,2,1024]{2,1,0:T(2,128)(2,1)S(1)} %reshape.525), channel_id=1, replica_groups=mesh['kv'=8,'pool'=64] {'pool'}, dimensions={0} | all-to-all | bytes 524288 | tf_op jit(solution)/shard_map/all_to_all | solution.py:146
  125.5 80.1 %all-gather = bf16[64,1,1024]{2,1,0:T(2,128)(2,1)S(1)} all-gather(bf16[1,1,1024]{2,1,0:T(2,128)(2,1)S(1)} %bitcast.110), channel_id=1, replica_groups=mesh['kv'=8,'pool'=64] {'pool'}, dimensions={0}, use_global_device_ids=true | all-gather | bytes 133120 | tf_op jit(solution)/shard_map/all_gather | solution.py:152
  205.8 23.6 %psum.15 = bf16[64,32]{0,1:T(8,128)(2,1)S(1)} all-reduce(f32[64,32]{0,1:T(8,128)S(1)} %fusion.19), channel_id=1, replica_groups=mesh['kv'=8,'pool'=64] {'kv'}, use_global_device_ids=true, to_apply=%region_10.11 | all-reduce | flops 2048 | bytes 12288 | tf_op jit(solution)/shard_map/psum | solution.py:156
  229.5 21.3 %all_to_all.53 = bf16[64,1,32]{2,1,0:T(2,128)(2,1)S(1)} all-to-all(bf16[64,1,32]{2,1,0:T(2,128)(2,1)S(1)} %copy.66), channel_id=1, replica_groups=mesh['kv'=8,'pool'=64] {'pool'}, dimensions={0} | all-to-all | bytes 8192 | tf_op jit(solution)/shard_map/all_to_all | solution.py:157
  251.0 0.6 add_convert_fusion
  (81 shorter events, 7.0 us)
Async XLA Ops:
  0.0 64.0 %copy-start = (bf16[256,2048]{1,0:T(8,128)(2,1)S(1)}, bf16[256,2048]{1,0:T(8,128)(2,1)}, u32[]{:S(2)}) copy-start(bf16[256,2048]{1,0:T(8,128)(2,1)} %param.16) | copy-start | bytes 3145732
  0.0 0.8 copy-start.4
  2.1 2.0 copy-start.7
  2.1 0.7 copy-start.1
  2.1 24.4 %copy-start.2 = (bf16[2,2048,128]{2,1,0:T(8,128)(2,1)S(1)}, bf16[2,2048,128]{2,1,0:T(8,128)(2,1)}, u32[]{:S(2)}) copy-start(bf16[2,2048,128]{2,1,0:T(8,128)(2,1)} %param.15) | copy-start | bytes 3145732
  4.1 22.4 %copy-start.9 = (s32[16]{0:T(128)S(1)}, s32[16]{0:T(128)}, u32[]{:S(2)}) copy-start(s32[16]{0:T(128)} %param.18) | copy-start | bytes 196
  5.6 22.8 %copy-start.3 = (bf16[2,16,128,128]{3,2,1,0:T(8,128)(2,1)S(1)}, bf16[2,16,128,128]{3,2,1,0:T(8,128)(2,1)}, u32[]{:S(2)}) copy-start(bf16[2,16,128,128]{3,2,1,0:T(8,128)(2,1)} %param.17) | copy-start | bytes 3145732
  7.8 32.2 %all-to-all-start = ((bf16[64,2,128]{2,1,0:T(2,128)(2,1)}), bf16[64,2,128]{2,1,0:T(2,128)(2,1)S(1)}, u32[]{:S(2)}, u32[]{:S(2)}) async-start(bf16[64,2,128]{2,1,0:T(2,128)(2,1)} %reshape.523), calls=%async_computation | async-start | bytes 65536 | tf_op jit(solution)/shard_map/all_to_all | solution.py:18
  27.7 0.7 copy-start.8
  42.5 20.0 %all-to-all-start.1 = ((f32[64,1,512]{2,1,0:T(1,128)}), f32[64,1,512]{2,1,0:T(1,128)S(1)}, u32[]{:S(2)}, u32[]{:S(2)}) async-start(f32[64,1,512]{2,1,0:T(1,128)} %all_to_all.44), calls=%async_computation.1 | async-start | bytes 262144 | tf_op jit(solution)/shard_map/all_to_all | solution.py:108
  78.4 20.8 %copy-start.5 = (bf16[32,1024]{1,0:T(8,128)(2,1)S(1)}, bf16[32,1024]{1,0:T(8,128)(2,1)}, u32[]{:S(2)}) copy-start(bf16[32,1024]{1,0:T(8,128)(2,1)} %param.22) | copy-start | bytes 196612
  99.2 0.9 copy-start.6
  125.5 80.1 %copy-start.10 = (bf16[1024,32]{0,1:T(8,128)(2,1)S(1)}, bf16[1024,32]{0,1:T(8,128)(2,1)}, u32[]{:S(2)}) copy-start(bf16[1024,32]{0,1:T(8,128)(2,1)} %param.23) | copy-start | bytes 196612
